TPU v7x, 256 devices: a whole 4x4x8 slice. The times are simulated.
256 devices in a mesh: tm: 32 (over x, z), tensor: 8 (over y, core).
Axes of the slice: x: 4, y: 4, z: 8, core: 2. Of those that a mesh axis runs over, the one named last changes fastest.
Arguments:
- latents: float32 [32, 640, 64], P('tm', 'tensor'), may hold values from -6 to 6
- residual: bfloat16 [32, 640, 5120], P('tm'), may hold values from -6 to 6
- timesteps: int32 [32], P('tm'), may hold values from 0 to 999
- step_sizes: float32 [32], P('tm'), may hold values from 0.015 to 0.06
- embed_weight: bfloat16 [64, 5120], replicated
- mod_weight: bfloat16 [3, 256, 5120], P(None, None, 'tensor'), may hold values from -0.75 to 0.75
- up_weight: bfloat16 [5120, 7168], P('tm', 'tensor'), may hold values from -0.078125 to 0.078125
- down_weight: bfloat16 [7168, 5120], P('tensor', 'tm'), may hold values from -0.0625 to 0.0625
- head_weight: bfloat16 [5120, 64], replicated, may hold values from -0.078125 to 0.078125
Outputs:
- drift: float32 [32, 640, 64], P('tm', 'tensor')
- new_latents: float32 [32, 640, 64], P('tm', 'tensor')
All inputs are finite; a program needn't handle non-finite values.
Results may differ from a plain program's by a relative error of at most 0.0085.
Values may be sent and summed in bfloat16 or wider, within the bound.
No kernel may reach another device: no remote copies, remote signals or barrier semaphores. Data moves between devices by JAX's collectives and lax.ppermute only.
A program may use at most 128 MiB of HBM per device.

v0:
```python
import math

import jax
import jax.numpy as jnp
from jax import lax
from jax.sharding import PartitionSpec as P


def prefix(part, axis, combine, identity):
    place = lax.axis_index(axis)
    gathered = lax.all_gather(part, axis)
    state = jnp.zeros_like(part) + jnp.asarray(identity, part.dtype)

    def one(hop, state):
        return combine(state, lax.dynamic_index_in_dim(gathered, hop, 0, False))

    return lax.fori_loop(0, place, one, state)


def normalize(values):
    centre = values - jnp.mean(values, axis=-1, keepdims=True)
    spread = jnp.mean(centre * centre, axis=-1, keepdims=True)
    return centre * lax.rsqrt(spread + 1e-06)


def time_features(stamps, width):
    half = width // 2
    freqs = jnp.exp(-math.log(10000.0) * jnp.arange(half, dtype=jnp.float32) / half)
    angles = stamps.astype(jnp.float32)[:, None] * freqs[None, :]
    return jnp.concatenate([jnp.cos(angles), jnp.sin(angles)], axis=-1)


def add_terms(earlier, later):
    return earlier + later


def local(
    latents,
    residual,
    timesteps,
    step_sizes,
    embed_weight,
    mod_weight,
    up_weight,
    down_weight,
    head_weight,
):
    feature = jax.nn.silu(time_features(timesteps, mod_weight.shape[1])).astype(jnp.bfloat16)[0]
    piece_mod = jnp.einsum("f,kfd->kd", feature, mod_weight, preferred_element_type=jnp.float32)
    modulation = lax.all_gather(piece_mod, "tensor", axis=1, tiled=True)
    latent = latents[0]
    stream = residual[0]
    latent_bf = latent.astype(jnp.bfloat16)
    own_rows = latent.shape[0]
    row_start = lax.axis_index("tensor") * own_rows
    own_stream = lax.dynamic_slice_in_dim(stream, row_start, own_rows, 0)
    hidden = own_stream.astype(jnp.float32) + jnp.dot(
        latent_bf, embed_weight, preferred_element_type=jnp.float32
    )
    local_normed = (normalize(hidden) * (1.0 + modulation[1]) + modulation[0]).astype(jnp.bfloat16)
    normed = lax.all_gather(local_normed, "tensor", axis=0, tiled=True)
    preact = jnp.dot(
        normed,
        lax.all_gather(up_weight, "tm", axis=0, tiled=True),
        preferred_element_type=jnp.float32,
    )
    activated = jax.nn.gelu(preact, approximate=True).astype(jnp.bfloat16)
    partial_sums = jnp.dot(
        activated,
        lax.all_gather(down_weight, "tm", axis=1, tiled=True),
        preferred_element_type=jnp.float32,
    )
    mixed = lax.psum_scatter(
        partial_sums.astype(jnp.bfloat16), "tensor", scatter_dimension=0, tiled=True
    ).astype(jnp.float32)
    updated = hidden + modulation[2] * mixed
    drift = jnp.dot(
        normalize(updated).astype(jnp.bfloat16), head_weight, preferred_element_type=jnp.float32
    )
    position = lax.axis_index("tm")
    first = (position == 0).astype(jnp.float32)
    term = first * latent - step_sizes[0] * drift
    earlier = prefix(term, "tm", add_terms, jnp.zeros_like(term))
    new_latent = earlier + term
    return (drift[None], new_latent[None])


def solution(mesh):
    in_specs = (
        P("tm", "tensor", None),
        P("tm", None, None),
        P("tm"),
        P("tm"),
        P(),
        P(None, None, "tensor"),
        P("tm", "tensor"),
        P("tensor", "tm"),
        P(),
    )
    out_specs = (P("tm", "tensor", None), P("tm", "tensor", None))
    return jax.shard_map(local, mesh=mesh, in_specs=in_specs, out_specs=out_specs, check_vma=False)
```

profile of v0, /device:TPU:6, one launch (start us, length us, event | category | flops | bytes accessed | tf_op | source)
XLA Modules:
  0.0 398.8 jit_solution(11767064728763271483)
XLA Ops:
  7.2 1.9 fusion.28
  9.2 0.3 multiply_reduce_fusion.1
  10.3 0.2 fusion.29
  10.5 13.3 %all_gather.18 = f32[3,5120]{1,0:T(4,128)S(1)} all-gather(f32[3,640]{1,0:T(4,128)S(1)} %bitcast.46), channel_id=1, replica_groups=mesh['tm'=32,'tensor'=8] {'tensor'}, dimensions={1}, use_global_device_ids=true | all-gather | bytes 69120 | tf_op jit(solution)/shard_map/all_gather | solution.py:50
  23.9 1.3 add_convert_fusion
  25.2 0.7 all-gather.8.cloned.1.call-update
  26.0 0.7 all-gather.10.cloned.1.call-update
  26.7 45.4 %all-gather.6.cloned.1.call-done = bf16[640,5120]{1,0:T(8,128)(2,1)} async-done(((bf16[80,5120]{1,0:T(8,128)(2,1)}), bf16[640,5120]{1,0:T(8,128)(2,1)}) %all-gather.6.cloned.1.call-update) | async-done | bytes 6553616 | tf_op jit(solution)/shard_map/all_gather | solution.py:61
  72.2 103.0 %all-gather.8.cloned.1.call-done = bf16[5120,896]{1,0:T(8,128)(2,1)} async-done(((bf16[160,896]{1,0:T(8,128)(2,1)}), bf16[5120,896]{1,0:T(8,128)(2,1)}) %all-gather.8.cloned.1.call-update) | async-done | bytes 9175056 | tf_op jit(solution)/shard_map/all_gather | solution.py:64
  175.2 12.7 %fusion.30 = f32[640,896]{1,0:T(8,128)} fusion(bf16[640,5120]{1,0:T(8,128)(2,1)} %all-gather.6.cloned.1.call-done, bf16[5120,896]{1,0:T(8,128)(2,1)} %all-gather.8.cloned.1.call-done), kind=kOutput, calls=%fused_computation.50 | convolution fusion | flops 5872025600 | bytes 18022400 | tf_op jit(solution)/shard_map/dot_general | solution.py:62
  187.9 89.2 %all-gather.10.cloned.1.call-done = bf16[896,5120]{0,1:T(8,128)(2,1)} async-done(((bf16[896,160]{0,1:T(8,128)(2,1)}), bf16[896,5120]{0,1:T(8,128)(2,1)}) %all-gather.10.cloned.1.call-update) | async-done | bytes 9175056 | tf_op jit(solution)/shard_map/all_gather | solution.py:70
  277.1 12.2 %convolution_convert_fusion = bf16[640,5120]{1,0:T(8,128)(2,1)} fusion(bf16[896,5120]{0,1:T(8,128)(2,1)} %all-gather.10.cloned.1.call-done, f32[640,896]{1,0:T(8,128)} %fusion.30), kind=kOutput, calls=%fused_computation.2 | convolution fusion | flops 5880463360 | bytes 18022400 | tf_op jit(solution)/shard_map/dot_general | solution.py:68
  289.9 44.7 %reduce-scatter.2.cloned.1.call-done = bf16[80,5120]{1,0:T(8,128)(2,1)} async-done(((bf16[640,5120]{1,0:T(8,128)(2,1)}), bf16[80,5120]{1,0:T(8,128)(2,1)}) %reduce-scatter.2.cloned.1.call-update) | async-done | bytes 819216 | tf_op jit(solution)/shard_map/reduce_scatter | solution.py:73
  334.6 1.5 fusion.16
  336.2 0.5 multiply_reduce_fusion
  336.7 0.6 copy-done.2
  337.3 0.6 fusion.13
  337.9 50.2 %all-gather.1 = f32[32,80,64]{1,2,0:T(8,128)S(1)} all-gather(f32[1,80,64]{1,2,0:T(8,128)S(1)} %fusion.19), channel_id=2, replica_groups=mesh['tm'=32,'tensor'=8] {'tm'}, dimensions={0}, use_global_device_ids=true | all-gather | bytes 675840 | tf_op jit(solution)/shard_map/all_gather | solution.py:11
  388.1 3.4 while.10
  388.2 0.1 copy.20
  388.3 0.1 copy.20
  388.4 0.1 copy.20
  389.0 0.1 copy.20
  391.6 0.6 add_bitcast_fusion
  (95 shorter events, 2.5 us)
Async XLA Ops:
  7.2 3.1 copy-start
  7.2 65.0 %all-gather.6.cloned.1.call-start = ((), (), s32[]{:S(2)}) async-start(), calls=%async_computation.1 | async-start | bytes 7372800 | tf_op jit(solution)/shard_map/all_gather | solution.py:61
  25.2 150.0 %all-gather.8.cloned.1.call-start = ((), (), s32[]{:S(2)}) async-start(), calls=%async_computation.2 | async-start | bytes 9461760 | tf_op jit(solution)/shard_map/all_gather | solution.py:64
  26.0 251.1 %all-gather.10.cloned.1.call-start = ((), (), s32[]{:S(2)}) async-start(), calls=%async_computation.3 | async-start | bytes 9461760 | tf_op jit(solution)/shard_map/all_gather | solution.py:70
  26.7 307.9 %reduce-scatter.2.cloned.1.call-start = ((), (), s32[]{:S(2)}) async-start(), calls=%async_computation.4 | async-start | bytes 7372800 | tf_op jit(solution)/shard_map/reduce_scatter | solution.py:73
  334.6 1.6 copy-start.1
  336.2 1.1 copy-start.2
  336.7 1.2 copy-start.3
  337.9 54.4 %copy-start.4 = (f32[80,64]{0,1:T(8,128)}, f32[80,64]{0,1:T(8,128)S(1)}, u32[]{:S(2)}) copy-start(f32[80,64]{0,1:T(8,128)S(1)} %fusion.13) | copy-start | bytes 61444
Sparse Core Ops, SparseCore 0:
  25.3 46.7 all-gather.5
  74.7 100.4 all-gather.7
  177.8 99.2 all-gather.9
  289.4 45.1 reduce-scatter.1
where the time goes:
time: 399 us
  waiting for transfers between devices  284 us (71%)
  blocking collectives  63.5 us (16%)
  matrix products  27.6 us (7%)
  between operations  15.2 us (4%)
  other arithmetic  4.66 us (1%)
    all_gather x1, waiting for transfers between devices, local(): lax.all_gather(up_weight, 'tm', axis=0, tiled=True)  103 us
    all_gather x1, waiting for transfers between devices, local(): lax.all_gather(down_weight, 'tm', axis=1, tiled=True)  89.2 us
    all_gather x1, blocking collectives, prefix(): gathered = lax.all_gather(part, axis)  50.2 us
    all_gather x1, waiting for transfers between devices, local(): normed = lax.all_gather(local_normed, 'tensor', axis=0, tiled=True)  45.4 us
    reduce_scatter x1, waiting for transfers between devices, local(): lax.psum_scatter(partial_sums.astype(jnp.bfloat16), 'tensor', scatter_dim...  44.7 us
    all_gather x1, blocking collectives, local(): modulation = lax.all_gather(piece_mod, 'tensor', axis=1, tiled=True)  13.3 us
    dot_general x1, matrix products, local(): jnp.dot(normed, lax.all_gather(up_weight, 'tm', axis=0, tiled=True), pref...  12.7 us
    dot_general x1, matrix products, local(): jnp.dot(activated, lax.all_gather(down_weight, 'tm', axis=1, tiled=True),...  12.2 us
  transfers between devices with their start and end apart: 4, of which 4 were waited for; matrix products, arithmetic and copies ran while one was open for 3% of the time, Pallas kernels for 0%

commit v1 on v0

v1 whole, which is shorter than its diff:
```python
import math

import jax
import jax.numpy as jnp
from jax import lax
from jax.sharding import PartitionSpec as P

STEPS = 32
CHUNKS = 4


def normalize(values):
    centre = values - jnp.mean(values, axis=-1, keepdims=True)
    spread = jnp.mean(centre * centre, axis=-1, keepdims=True)
    return centre * lax.rsqrt(spread + 1e-06)


def time_features(stamps, width):
    half = width // 2
    freqs = jnp.exp(-math.log(10000.0) * jnp.arange(half, dtype=jnp.float32) / half)
    angles = stamps.astype(jnp.float32)[:, None] * freqs[None, :]
    return jnp.concatenate([jnp.cos(angles), jnp.sin(angles)], axis=-1)


def running_sum(term):
    state = term
    hop = 1
    while hop < STEPS:
        pairs = [(i, i + hop) for i in range(STEPS - hop)]
        state = state + lax.ppermute(state, "tm", pairs)
        hop *= 2
    return state


def local(
    latents,
    residual,
    timesteps,
    step_sizes,
    embed_weight,
    mod_weight,
    up_weight,
    down_weight,
    head_weight,
):
    latent = latents[0]
    stream = residual[0]
    own_rows, channels = latent.shape
    width = stream.shape[1]
    depth = up_weight.shape[0]
    hidden_units = up_weight.shape[1]
    both = jnp.concatenate([up_weight, down_weight.T], axis=0)
    weights = lax.all_gather(both, "tm", axis=0)

    feature = jax.nn.silu(time_features(timesteps, mod_weight.shape[1])).astype(jnp.bfloat16)[0]
    piece_mod = jnp.einsum("f,kfd->kd", feature, mod_weight, preferred_element_type=jnp.float32)
    own = jnp.concatenate([piece_mod.reshape(-1), latent.reshape(-1)]).reshape(-1, 128)
    shared = lax.all_gather(own, "tensor", axis=0).reshape(8, -1)
    cut = piece_mod.size
    modulation = shared[:, :cut].reshape(8, 3, -1).transpose(1, 0, 2).reshape(3, width)
    all_latent = shared[:, cut:].reshape(8 * own_rows, channels)

    base = stream.astype(jnp.float32) + jnp.dot(
        all_latent.astype(jnp.bfloat16), embed_weight, preferred_element_type=jnp.float32
    )
    normed = (normalize(base) * (1.0 + modulation[1]) + modulation[0]).astype(jnp.bfloat16)

    row_start = lax.axis_index("tensor") * own_rows
    own_stream = lax.dynamic_slice_in_dim(stream, row_start, own_rows, 0)
    hidden = own_stream.astype(jnp.float32) + jnp.dot(
        latent.astype(jnp.bfloat16), embed_weight, preferred_element_type=jnp.float32
    )

    up = weights[:, :depth].reshape(width, hidden_units)
    preact = jnp.dot(normed, up, preferred_element_type=jnp.float32)
    activated = jax.nn.gelu(preact, approximate=True).astype(jnp.bfloat16)
    pieces = []
    per = STEPS // CHUNKS
    for c in range(CHUNKS):
        rows = weights[c * per : (c + 1) * per, depth:].reshape(per * depth, hidden_units)
        partial_sums = lax.dot_general(
            activated, rows, (((1,), (1,)), ((), ())), preferred_element_type=jnp.float32
        ).astype(jnp.bfloat16)
        pieces.append(lax.psum_scatter(partial_sums, "tensor", scatter_dimension=0, tiled=True))
    mixed = jnp.concatenate(pieces, axis=1).astype(jnp.float32)
    updated = hidden + modulation[2] * mixed
    drift = jnp.dot(
        normalize(updated).astype(jnp.bfloat16), head_weight, preferred_element_type=jnp.float32
    )
    first = (lax.axis_index("tm") == 0).astype(jnp.float32)
    new_latent = running_sum(first * latent - step_sizes[0] * drift)
    return (drift[None], new_latent[None])


def solution(mesh):
    in_specs = (
        P("tm", "tensor", None),
        P("tm", None, None),
        P("tm"),
        P("tm"),
        P(),
        P(None, None, "tensor"),
        P("tm", "tensor"),
        P("tensor", "tm"),
        P(),
    )
    out_specs = (P("tm", "tensor", None), P("tm", "tensor", None))
    return jax.shard_map(local, mesh=mesh, in_specs=in_specs, out_specs=out_specs, check_vma=False)
```

time: 399 us -> 387 us (0.970)
  blocking collectives: 63.5 us -> 13.3 us
  local copies, waits for them, and re-layouts: 2.8 us -> 23 us
  starting transfers between devices: 0.16 us -> 14.7 us
  matrix products: 27.6 us -> 36.6 us
  waiting for transfers between devices: 284 us -> 280 us
    all_gather x3 -> x1, waiting for transfers between devices: 238 us -> 124 us  [local(): weights = lax.all_gather(both, 'tm', axis=0)]
    reduce_scatter x1 -> x4, waiting for transfers between devices: 44.7 us -> 129 us  [local(): lax.psum_scatter(partial_sums, 'tensor', scatter_dimension=0, tiled=True)]
    all_gather x2 -> x1, blocking collectives: 63.5 us -> 13.3 us  [local(): shared = lax.all_gather(own, 'tensor', axis=0).reshape(8, -1)]
    ppermute x0 -> x5, waiting for transfers between devices: none -> 26.1 us  [running_sum(): state = state + lax.ppermute(state, 'tm', pairs)]
    ppermute x0 -> x5, starting transfers between devices: none -> 14.3 us  [running_sum(): state = state + lax.ppermute(state, 'tm', pairs)]
    slice x0 -> x4, local copies, waits for them, and re-layouts: none -> 13.5 us  [the longest x1 7.83 us: local(): up = weights[:, :depth].reshape(width, hidden_units)]
    unnamed x10 -> x17, local copies, waits for them, and re-layouts: 0.6 us -> 9.29 us
    dot_general x3 -> x7, matrix products: 26.8 us -> 35.1 us  [the longest x4 17.6 us: local(): lax.dot_general(activated, rows, (((1,), (1,)), ((), ())), preferred_elem...]
  transfers between devices with their start and end apart: 4 -> 10, of which waited for: 4 -> 10; matrix products, arithmetic and copies ran while one was open for 3% -> 6% of each run, Pallas kernels for 0% -> 0%
where the time goes in v1:
time: 387 us
  waiting for transfers between devices  280 us (72%)
  matrix products  36.6 us (9%)
  local copies, waits for them, and re-layouts  23 us (6%)
  between operations  15.3 us (4%)
  starting transfers between devices  14.7 us (4%)
  blocking collectives  13.3 us (3%)
  other arithmetic  4.54 us (1%)
    reduce_scatter x4, waiting for transfers between devices, local(): lax.psum_scatter(partial_sums, 'tensor', scatter_dimension=0, tiled=True)  129 us
    all_gather x1, waiting for transfers between devices, local(): weights = lax.all_gather(both, 'tm', axis=0)  124 us
    ppermute x5, waiting for transfers between devices, running_sum(): state = state + lax.ppermute(state, 'tm', pairs)  26.1 us
    dot_general x4, matrix products, local(): lax.dot_general(activated, rows, (((1,), (1,)), ((), ())), preferred_elem...  17.6 us
    ppermute x5, starting transfers between devices, running_sum(): state = state + lax.ppermute(state, 'tm', pairs)  14.3 us
    all_gather x1, blocking collectives, local(): shared = lax.all_gather(own, 'tensor', axis=0).reshape(8, -1)  13.3 us
    dot_general x1, matrix products, local(): preact = jnp.dot(normed, up, preferred_element_type=jnp.float32)  10.2 us
    unnamed x17, local copies, waits for them, and re-layouts  9.29 us
  transfers between devices with their start and end apart: 10, of which 10 were waited for; matrix products, arithmetic and copies ran while one was open for 6% of the time, Pallas kernels for 0%

profile of v1, /device:TPU:6, one launch (start us, length us, event | category | flops | bytes accessed | tf_op | source)
XLA Modules:
  0.0 387.0 jit_solution(1940872317737962322)
XLA Ops:
  12.1 13.3 %all_gather.9 = f32[8,55,128]{2,1,0:T(8,128)S(1)} all-gather(f32[1,55,128]{2,1,0:T(8,128)S(1)} %maximum_bitcast_fusion), channel_id=1, replica_groups=mesh['tm'=32,'tensor'=8] {'tensor'}, dimensions={0}, use_global_device_ids=true | all-gather | bytes 253440 | tf_op jit(solution)/shard_map/all_gather | solution.py:58
  25.7 5.2 %fusion.24 = (f32[640]{0:T(1024)S(1)}, f32[640,5120]{1,0:T(8,128)S(1)}) fusion(bf16[640,64]{1,0:T(8,128)(2,1)S(1)} %convert_element_type.66, bf16[64,5120]{1,0:T(8,128)(2,1)S(1)} %copy-done, bf16[1,640,5120]{2,1,0:T(8,128)(2,1)} %param.10), kind=kOutput, calls=%fused_computation.50 | convolution fusion | flops 429260160 | bytes 20400640 | tf_op jit(solution)/shard_map/dot_general | solution.py:63
  32.3 3.3 copy-done.1
  35.6 124.4 %all-gather.3.cloned.1.call-done = bf16[10240,896]{1,0:T(8,128)(2,1)} async-done(((bf16[320,896]{1,0:T(8,128)(2,1)}), bf16[10240,896]{1,0:T(8,128)(2,1)}) %all-gather.3.cloned.1.call-update) | async-done | bytes 18350096 | tf_op jit(solution)/shard_map/all_gather | solution.py:53
  160.0 7.8 %slice.49 = bf16[32,160,896]{2,1,0:T(8,128)(2,1)} slice(bf16[32,320,896]{2,1,0:T(8,128)(2,1)} %bitcast.53), slice={[0:32], [0:160], [0:896]} | slice | bytes 18350080 | tf_op jit(solution)/shard_map/slice | solution.py:74
  167.8 5.6 %fusion.22 = (bf16[8,160,896]{2,1,0:T(8,128)(2,1)S(1)}, bf16[8,160,896]{2,1,0:T(8,128)(2,1)S(1)}, bf16[8,160,896]{2,1,0:T(8,128)(2,1)}, bf16[8,160,896]{2,1,0:T(8,128)(2,1)}) fusion(bf16[32,320,896]{2,1,0:T(8,128)(2,1)} %bitcast.54), kind=kLoop, calls=%fused_computation.48 | loop fusion | bytes 18350080 | tf_op jit(solution)/shard_map/slice | solution.py:80
  173.5 3.4 copy-done.2
  176.9 10.2 %fusion.13 = bf16[640,896]{1,0:T(8,128)(2,1)S(1)} fusion(bf16[5120,896]{1,0:T(8,128)(2,1)} %bitcast.55, f32[640,5120]{1,0:T(8,128)S(1)} %copy-done.2, f32[5120]{0:T(1024)S(1)} %add.105, f32[5120]{0:T(1024)S(1)} %add.104, f32[640]{0:T(1024)S(1)} %add_rsqrt_fusion, f32[640]{0:T(1024)S(1)} %broadcast_multiply_fusion), kind=kOutput, calls=%fused_computation.22 | convolution fusion | flops 5893570560 | bytes 23475200 | tf_op jit(solution)/shard_map/dot_general | solution.py:75
  188.2 3.1 convolution_convert_fusion.3
  191.5 5.1 %convolution_convert_fusion.2 = bf16[640,1280]{1,0:T(8,128)(2,1)} fusion(bf16[640,896]{1,0:T(8,128)(2,1)} %copy-done.6, bf16[1280,896]{1,0:T(8,128)(2,1)} %bitcast.59), kind=kOutput, calls=%fused_computation.13 | convolution fusion | flops 1468825600 | bytes 5079040 | tf_op jit(solution)/shard_map/dot_general | solution.py:81
  196.6 5.1 %convolution_convert_fusion.1 = bf16[640,1280]{1,0:T(8,128)(2,1)} fusion(bf16[640,896]{1,0:T(8,128)(2,1)} %copy-done.6, bf16[1280,896]{1,0:T(8,128)(2,1)} %bitcast.58), kind=kOutput, calls=%fused_computation.12 | convolution fusion | flops 1468825600 | bytes 5079040 | tf_op jit(solution)/shard_map/dot_general | solution.py:81
  201.8 4.4 %convolution_convert_fusion = bf16[640,1280]{1,0:T(8,128)(2,1)} fusion(bf16[640,896]{1,0:T(8,128)(2,1)} %copy-done.6, bf16[1280,896]{1,0:T(8,128)(2,1)S(1)} %bitcast.57), kind=kOutput, calls=%fused_computation.11 | convolution fusion | flops 1468825600 | bytes 5079040 | tf_op jit(solution)/shard_map/dot_general | solution.py:81
  206.9 18.8 %reduce-scatter.5.cloned.1.call-done = bf16[80,1280]{1,0:T(8,128)(2,1)} async-done(((bf16[640,1280]{1,0:T(8,128)(2,1)}), bf16[80,1280]{1,0:T(8,128)(2,1)}) %reduce-scatter.5.cloned.1.call-update) | async-done | bytes 204816 | tf_op jit(solution)/shard_map/reduce_scatter | solution.py:84
  225.7 36.8 %reduce-scatter.7.cloned.1.call-done = bf16[80,1280]{1,0:T(8,128)(2,1)} async-done(((bf16[640,1280]{1,0:T(8,128)(2,1)}), bf16[80,1280]{1,0:T(8,128)(2,1)}) %reduce-scatter.7.cloned.1.call-update) | async-done | bytes 204816 | tf_op jit(solution)/shard_map/reduce_scatter | solution.py:84
  262.5 36.7 %reduce-scatter.9.cloned.1.call-done = bf16[80,1280]{1,0:T(8,128)(2,1)} async-done(((bf16[640,1280]{1,0:T(8,128)(2,1)}), bf16[80,1280]{1,0:T(8,128)(2,1)}) %reduce-scatter.9.cloned.1.call-update) | async-done | bytes 204816 | tf_op jit(solution)/shard_map/reduce_scatter | solution.py:84
  299.2 36.6 %reduce-scatter.11.cloned.1.call-done = bf16[80,1280]{1,0:T(8,128)(2,1)} async-done(((bf16[640,1280]{1,0:T(8,128)(2,1)}), bf16[80,1280]{1,0:T(8,128)(2,1)}) %reduce-scatter.11.cloned.1.call-update) | async-done | bytes 204816 | tf_op jit(solution)/shard_map/reduce_scatter | solution.py:84
  339.4 3.5 collective-permute-start
  342.9 4.4 %collective-permute-done = f32[80,64]{0,1:T(8,128)S(1)} collective-permute-done((f32[80,64]{0,1:T(8,128)S(1)}, f32[80,64]{0,1:T(8,128)S(1)}, u32[]{:S(2)}, u32[]{:S(2)}) %collective-permute-start) | collective-permute-done | bytes 20512 | tf_op jit(solution)/shard_map/ppermute | solution.py:30
  347.3 2.3 collective-permute-start.1
  349.7 6.5 %collective-permute-done.1 = f32[80,64]{0,1:T(8,128)S(1)} collective-permute-done((f32[80,64]{0,1:T(8,128)S(1)}, f32[80,64]{0,1:T(8,128)S(1)}, u32[]{:S(2)}, u32[]{:S(2)}) %collective-permute-start.1) | collective-permute-done | bytes 20512 | tf_op jit(solution)/shard_map/ppermute | solution.py:30
  356.1 5.9 %collective-permute-start.2 = (f32[80,64]{0,1:T(8,128)S(1)}, f32[80,64]{0,1:T(8,128)S(1)}, u32[]{:S(2)}, u32[]{:S(2)}) collective-permute-start(f32[80,64]{0,1:T(8,128)S(1)} %add.115), channel_id=1, source_target_pairs={{0,32},{8,40},{16,48},{24,56},{32,64},{40,72},{48,80},{56,88},{64,... | collective-permute-start | bytes 61448 | tf_op jit(solution)/shard_map/ppermute | solution.py:30
  362.0 4.7 %collective-permute-done.2 = f32[80,64]{0,1:T(8,128)S(1)} collective-permute-done((f32[80,64]{0,1:T(8,128)S(1)}, f32[80,64]{0,1:T(8,128)S(1)}, u32[]{:S(2)}, u32[]{:S(2)}) %collective-permute-start.2) | collective-permute-done | bytes 20512 | tf_op jit(solution)/shard_map/ppermute | solution.py:30
  368.0 4.5 %collective-permute-done.3 = f32[80,64]{0,1:T(8,128)S(1)} collective-permute-done((f32[80,64]{0,1:T(8,128)S(1)}, f32[80,64]{0,1:T(8,128)S(1)}, u32[]{:S(2)}, u32[]{:S(2)}) %collective-permute-start.3) | collective-permute-done | bytes 20512 | tf_op jit(solution)/shard_map/ppermute | solution.py:30
  373.8 6.0 %collective-permute-done.4 = f32[80,64]{0,1:T(8,128)S(1)} collective-permute-done((f32[80,64]{0,1:T(8,128)S(1)}, f32[80,64]{0,1:T(8,128)S(1)}, u32[]{:S(2)}, u32[]{:S(2)}) %collective-permute-start.4) | collective-permute-done | bytes 20512 | tf_op jit(solution)/shard_map/ppermute | solution.py:30
  (54 shorter events, 14.0 us)
Async XLA Ops:
  7.2 18.5 %copy-start = (bf16[64,5120]{1,0:T(8,128)(2,1)S(1)}, bf16[64,5120]{1,0:T(8,128)(2,1)}, u32[]{:S(2)}) copy-start(bf16[64,5120]{1,0:T(8,128)(2,1)} %param.13) | copy-start | bytes 1966084
  7.2 3.8 copy-start.3
  7.2 152.8 %all-gather.3.cloned.1.call-start = ((), (), s32[]{:S(2)}) async-start(), calls=%async_computation.8 | async-start | bytes 18923520 | tf_op jit(solution)/shard_map/all_gather | solution.py:53
  9.3 216.4 %reduce-scatter.5.cloned.1.call-start = ((), (), s32[]{:S(2)}) async-start(), calls=%async_computation.4 | async-start | bytes 1843200 | tf_op jit(solution)/shard_map/reduce_scatter | solution.py:84
  30.8 4.7 %copy-start.1 = (f32[640,5120]{1,0:T(8,128)}, f32[640,5120]{1,0:T(8,128)S(1)}, u32[]{:S(2)}) copy-start(f32[640,5120]{1,0:T(8,128)S(1)} %get-tuple-element.10) | copy-start | bytes 39321604
  167.8 9.1 %copy-start.2 = (f32[640,5120]{1,0:T(8,128)S(1)}, f32[640,5120]{1,0:T(8,128)}, u32[]{:S(2)}) copy-start(f32[640,5120]{1,0:T(8,128)} %copy-done.1) | copy-start | bytes 39321604
  187.2 1.0 copy-start.6
  191.2 71.3 %reduce-scatter.7.cloned.1.call-start = ((), (), s32[]{:S(2)}) async-start(), calls=%async_computation.5 | async-start | bytes 1843200 | tf_op jit(solution)/shard_map/reduce_scatter | solution.py:84
  196.6 102.6 %reduce-scatter.9.cloned.1.call-start = ((), (), s32[]{:S(2)}) async-start(), calls=%async_computation.6 | async-start | bytes 1843200 | tf_op jit(solution)/shard_map/reduce_scatter | solution.py:84
  201.7 134.1 %reduce-scatter.11.cloned.1.call-start = ((), (), s32[]{:S(2)}) async-start(), calls=%async_computation.7 | async-start | bytes 1843200 | tf_op jit(solution)/shard_map/reduce_scatter | solution.py:84
  201.8 134.1 %copy-start.5 = (f32[1,80,64]{1,2,0:T(8,128)S(1)}, f32[1,80,64]{1,2,0:T(8,128)}, u32[]{:S(2)}) copy-start(f32[1,80,64]{1,2,0:T(8,128)} %param.9) | copy-start | bytes 61444
  206.9 131.5 %copy-start.4 = (bf16[5120,64]{0,1:T(8,128)(2,1)S(1)}, bf16[5120,64]{0,1:T(8,128)(2,1)}, u32[]{:S(2)}) copy-start(bf16[5120,64]{0,1:T(8,128)(2,1)} %param.17) | copy-start | bytes 1966084
  339.4 7.9 %collective-permute-start = (f32[80,64]{0,1:T(8,128)S(1)}, f32[80,64]{0,1:T(8,128)S(1)}, u32[]{:S(2)}, u32[]{:S(2)}) collective-permute-start(f32[80,64]{0,1:T(8,128)S(1)} %get-tuple-element.13), channel_id=1, source_target_pairs={{0,8},{8,16},{16,24},{24,32},{32,40},{40,48},{48,56},{56,64},{64,7... | collective-permute-start | bytes 61448 | tf_op jit(solution)/shard_map/ppermute | solution.py:30
  347.3 8.8 %collective-permute-start.1 = (f32[80,64]{0,1:T(8,128)S(1)}, f32[80,64]{0,1:T(8,128)S(1)}, u32[]{:S(2)}, u32[]{:S(2)}) collective-permute-start(f32[80,64]{0,1:T(8,128)S(1)} %add.114), channel_id=1, source_target_pairs={{0,16},{8,24},{16,32},{24,40},{32,48},{40,56},{48,64},{56,72},{64,... | collective-permute-start | bytes 61448 | tf_op jit(solution)/shard_map/ppermute | solution.py:30
  356.1 10.6 %collective-permute-start.2 = (f32[80,64]{0,1:T(8,128)S(1)}, f32[80,64]{0,1:T(8,128)S(1)}, u32[]{:S(2)}, u32[]{:S(2)}) collective-permute-start(f32[80,64]{0,1:T(8,128)S(1)} %add.115), channel_id=1, source_target_pairs={{0,32},{8,40},{16,48},{24,56},{32,64},{40,72},{48,80},{56,88},{64,... | collective-permute-start | bytes 61448 | tf_op jit(solution)/shard_map/ppermute | solution.py:30
  366.7 5.8 %collective-permute-start.3 = (f32[80,64]{0,1:T(8,128)S(1)}, f32[80,64]{0,1:T(8,128)S(1)}, u32[]{:S(2)}, u32[]{:S(2)}) collective-permute-start(f32[80,64]{0,1:T(8,128)S(1)} %add.116), channel_id=1, source_target_pairs={{0,64},{8,72},{16,80},{24,88},{32,96},{40,104},{48,112},{56,120},{... | collective-permute-start | bytes 61448 | tf_op jit(solution)/shard_map/ppermute | solution.py:30
  372.5 7.3 %collective-permute-start.4 = (f32[80,64]{0,1:T(8,128)S(1)}, f32[80,64]{0,1:T(8,128)S(1)}, u32[]{:S(2)}, u32[]{:S(2)}) collective-permute-start(f32[80,64]{0,1:T(8,128)S(1)} %add.117), channel_id=1, source_target_pairs={{0,128},{8,136},{16,144},{24,152},{32,160},{40,168},{48,176},{56,1... | collective-permute-start | bytes 61448 | tf_op jit(solution)/shard_map/ppermute | solution.py:30
Sparse Core Ops, SparseCore 0:
  10.6 149.3 all-gather.2
  191.4 34.3 reduce-scatter.4
  228.3 34.1 reduce-scatter.6
  264.9 34.1 reduce-scatter.8
  301.6 34.1 reduce-scatter.10
